TPU v7x, 128 devices: a whole 4x4x4 slice. The times are simulated.
128 devices in a mesh: gx: 16 (over z, y), gy: 8 (over x, core).
Axes of the slice: x: 4, y: 4, z: 4, core: 2. Of those that a mesh axis runs over, the one named last changes fastest.
Arguments:
- state: float32 [512, 512, 128], P('gx', 'gy'), may hold values from -6 to 6
- syndromes: int32 [2, 512, 512], P(None, 'gx', 'gy'), may hold values from 0 to 1
- erased: int32 [2, 128, 128], P(None, 'gx', 'gy'), may hold values 0 or 1
- readers: int32 [16384, 1], P(('gx', 'gy')), may hold values from 0 to 127; in each aligned block of 128 rows (0 to 127, 128 to 255, ...) at most 2 rows name the same one
- conv_weight: float32 [9, 128, 128], replicated, may hold values from -0.1875 to 0.1875
- syndrome_table: float32 [2, 128], replicated, may hold values from -6 to 6
- erasure_vector: float32 [128], replicated, may hold values from -6 to 6
- read_weight: float32 [16384, 128], P(('gx', 'gy')), may hold values from -0.5 to 0.5
- erasure_offset: float32 [128], replicated, may hold values from -6 to 6
Outputs:
- final_state: float32 [512, 512, 128], P('gx', 'gy')
Inputs may be any that keep to these rules, and one draw needn't show every extreme that they name: `readers`: among the 128 blocks of one device no reader is named more than 2 times, a bound that some block reaches.
All inputs are finite; a program needn't handle non-finite values. No bound on the sum of `erased` on one device may be relied on, other than what follows from the above.
Results may differ from a plain program's by a relative error of at most 0.0003.
Values sent between devices are 32-bit elements; how exact they have to be, the bound alone decides.
No kernel may reach another device: no remote copies, remote signals or barrier semaphores. Data moves between devices by JAX's collectives and lax.ppermute only.
A program may use at most 64 MiB of HBM per device.

v0:
```python
import jax
import jax.numpy as jnp
from jax import lax
from jax.sharding import PartitionSpec as P

BS = 4
ROUNDS = 2
precise = lax.Precision.HIGHEST


def padded_2(cells, sides, width):
    for axis, dim in sides:
        count = lax.axis_size(axis)
        ends = count - 1
        head = lax.slice_in_dim(cells, 0, width, axis=dim)
        tail = lax.slice_in_dim(cells, cells.shape[dim] - width, cells.shape[dim], axis=dim)
        cells = jnp.concatenate(
            [
                lax.ppermute(tail, axis, [(i, (i + 1) % count) for i in range(ends)]),
                cells,
                lax.ppermute(head, axis, [((i + 1) % count, i) for i in range(ends)]),
            ],
            axis=dim,
        )
    return cells


def to_blocks(field, block_side):
    row_count, col_count, channels = field.shape
    block_grid = field.reshape(
        row_count // block_side, block_side, col_count // block_side, block_side, channels
    )
    return block_grid.transpose(0, 2, 1, 3, 4).reshape(
        row_count // block_side * (col_count // block_side), block_side * block_side * channels
    )


def spread_cells(values, block_rows, block_cols, block_side):
    width = values.shape[-1]
    block_grid = values.reshape(block_rows, 1, block_cols, 1, width)
    return jnp.broadcast_to(
        block_grid, (block_rows, block_side, block_cols, block_side, width)
    ).reshape(block_rows * block_side, block_cols * block_side, width)


def reader_head(payload, flag_vals, weight, offset, form):
    channels = offset.shape[0]
    lead_shape = payload.shape[:-1]
    cell_vals = payload.reshape(lead_shape + (payload.shape[-1] // channels, channels))
    mixed_vals = jnp.tanh(jnp.einsum(form, cell_vals, weight, precision=precise))
    pooled = jnp.mean(mixed_vals, axis=-2)
    return jnp.tanh(pooled + flag_vals[..., None] * offset)


def per_device(
    state,
    syndromes,
    erased,
    readers,
    conv_weight,
    syndrome_table,
    erasure_vector,
    read_weight,
    erasure_offset,
):
    tile_rows, tile_cols, channels = state.shape
    block_side = BS
    block_rows = tile_rows // block_side
    block_cols = tile_cols // block_side
    block_count = block_rows * block_cols
    gx_count = lax.axis_size("gx")
    gy_count = lax.axis_size("gy")
    device_count = gx_count * gy_count
    reader_ids = readers[:, 0]
    all_weights = lax.all_gather(read_weight, ("gx", "gy"), axis=0, tiled=True)
    block_weights = all_weights.reshape(device_count, channels, channels)[reader_ids]
    field = state
    for round_index in range(ROUNDS):
        block_flags = erased[round_index].reshape(block_count).astype(jnp.float32)
        block_states = to_blocks(field, block_side)
        corrections = reader_head(
            block_states, block_flags, block_weights, erasure_offset, "bpc,bcd->bpd"
        )
        correction_cells = spread_cells(corrections, block_rows, block_cols, block_side)
        padded = padded_2(field, (("gx", 0), ("gy", 1)), 1)
        conv_sum = jnp.zeros((tile_rows * tile_cols, channels), jnp.float32)
        for tap_index in range(9):
            row_off = tap_index // 3
            col_off = tap_index % 3
            shifted = padded[row_off : row_off + tile_rows, col_off : col_off + tile_cols].reshape(
                -1, channels
            )
            conv_sum = conv_sum + jnp.dot(
                shifted,
                conv_weight[tap_index],
                precision=precise,
                preferred_element_type=jnp.float32,
            )
        conv_sum = conv_sum.reshape(tile_rows, tile_cols, channels)
        erased_cells = spread_cells(
            erased[round_index][:, :, None], block_rows, block_cols, block_side
        )
        bits = syndromes[round_index][:, :, None]
        inputs = jnp.where(
            erased_cells > 0,
            erasure_vector,
            jnp.where(bits == 1, syndrome_table[1], syndrome_table[0]),
        )
        field = 0.5 * field + jnp.tanh(conv_sum + inputs + correction_cells)
    return field


def solution(mesh):
    placed = (
        P("gx", "gy", None),
        P(None, "gx", "gy"),
        P(None, "gx", "gy"),
        P(("gx", "gy"), None),
        P(),
        P(),
        P(),
        P(("gx", "gy"), None),
        P(),
    )
    return jax.shard_map(
        per_device, mesh=mesh, in_specs=placed, out_specs=P("gx", "gy", None), check_vma=False
    )
```

profile of v0, /device:TPU:33, one launch (start us, length us, event | category | flops | bytes accessed | tf_op | source)
XLA Modules:
  0.0 146.4 jit_solution(11949596468125509112)
XLA Ops:
  6.5 0.7 all-gather.2.cloned.1.call-update
  7.3 0.8 fusion.57
  8.0 3.2 %collective-permute-start = (f32[1,64,128]{2,1,0:T(8,128)S(1)}, f32[1,64,128]{2,1,0:T(8,128)S(1)}, u32[]{:S(2)}, u32[]{:S(2)}) collective-permute-start(f32[1,64,128]{2,1,0:T(8,128)S(1)} %get-tuple-element.34), channel_id=1, source_target_pairs={{0,8},{8,16},{16,24},{24,32},{32,40},{40,48},{48,56},{56,64},{64,7... | collective-permute-start | bytes 98312 | tf_op jit(solution)/shard_map/ppermute | solution.py:19
  11.2 4.2 %collective-permute-start.1 = (f32[1,64,128]{2,1,0:T(8,128)S(1)}, f32[1,64,128]{2,1,0:T(8,128)S(1)}, u32[]{:S(2)}, u32[]{:S(2)}) collective-permute-start(f32[1,64,128]{2,1,0:T(8,128)S(1)} %get-tuple-element.33), channel_id=1, source_target_pairs={{8,0},{16,8},{24,16},{32,24},{40,32},{48,40},{56,48},{64,56},{72,6... | collective-permute-start | bytes 98312 | tf_op jit(solution)/shard_map/ppermute | solution.py:21
  15.4 0.7 fusion.52
  16.1 0.8 slice_bitcast_fusion.1
  16.9 0.7 compare_bitcast_fusion
  17.6 0.8 convert_bitcast_fusion
  18.4 0.7 fusion.51
  19.1 1.4 copy.12
  20.5 0.1 broadcast_in_dim.66
  20.6 0.2 gt.32
  20.8 0.1 broadcast_in_dim.73
  20.9 0.2 gt.35
  21.1 0.0 collective-permute-done
  21.1 0.0 copy-start.2
  21.1 0.4 pad_maximum_fusion.6
  21.5 4.2 %collective-permute-start.2 = (f32[34,1,128]{2,1,0:T(1,128)S(1)}, f32[34,1,128]{2,1,0:T(1,128)S(1)}, u32[]{:S(2)}, u32[]{:S(2)}) collective-permute-start(f32[34,1,128]{2,1,0:T(1,128)S(1)} %get-tuple-element.24), channel_id=1, source_target_pairs={{0,1},{1,2},{2,3},{3,4},{4,5},{5,6},{6,7},{8,9},{9,10},{10,11},{11... | collective-permute-start | bytes 52232 | tf_op jit(solution)/shard_map/ppermute | solution.py:19
  25.8 1.9 %collective-permute-start.3 = (f32[34,1,128]{2,1,0:T(1,128)S(1)}, f32[34,1,128]{2,1,0:T(1,128)S(1)}, u32[]{:S(2)}, u32[]{:S(2)}) collective-permute-start(f32[34,1,128]{2,1,0:T(1,128)S(1)} %get-tuple-element.25), channel_id=1, source_target_pairs={{1,0},{2,1},{3,2},{4,3},{5,4},{6,5},{7,6},{9,8},{10,9},{11,10},{12... | collective-permute-start | bytes 52232 | tf_op jit(solution)/shard_map/ppermute | solution.py:21
  27.7 1.0 fusion.14
  28.7 1.0 fusion.28
  29.7 1.6 %collective-permute-done.3 = f32[34,1,128]{2,1,0:T(1,128)S(1)} collective-permute-done((f32[34,1,128]{2,1,0:T(1,128)S(1)}, f32[34,1,128]{2,1,0:T(1,128)S(1)}, u32[]{:S(2)}, u32[]{:S(2)}) %collective-permute-start.3) | collective-permute-done | bytes 17440 | tf_op jit(solution)/shard_map/ppermute | solution.py:21
  31.3 0.9 pad_maximum_fusion.5
  32.2 1.0 fusion.11
  33.2 1.0 convolution_add_fusion.12
  34.2 1.0 convolution_add_fusion.11
  35.2 1.0 convolution_add_fusion.10
  36.2 1.0 convolution_add_fusion.9
  37.2 1.0 convolution_add_fusion.8
  38.2 1.1 fusion.2
  39.2 41.7 %all-gather.2.cloned.1.call-done = f32[16384,128]{1,0:T(8,128)} async-done(((f32[128,128]{1,0:T(8,128)}), f32[16384,128]{1,0:T(8,128)}) %all-gather.2.cloned.1.call-update) | async-done | bytes 8388624 | tf_op jit(solution)/shard_map/all_gather | solution.py:75
  81.0 7.7 %gather_fusion = f32[128,128,128]{2,1,0:T(8,128)} fusion(f32[128,128,128]{2,1,0:T(8,128)} %bitcast.126, s32[1024]{0:T(1024)S(1)} %pad_clamp_fusion), kind=kCustom, calls=%fused_computation | custom fusion | bytes 16777728 | tf_op jit(solution)/shard_map/gather | solution.py:76
  88.7 10.5 %fusion.3 = f32[128,128]{1,0:T(8,128)S(1)} fusion(f32[128,128,128]{2,1,0:T(8,128)} %gather_fusion, f32[128,16,128]{2,1,0:T(8,128)S(1)} %bitcast.132), kind=kOutput, calls=%fused_computation.29 | convolution fusion | flops 402898944 | bytes 9502720 | tf_op jit(solution)/shard_map/bpc,bcd->bpd/dot_general | solution.py:50
  99.2 0.0 copy-start.5
  99.2 0.1 add_tanh_fusion.1
  99.3 0.2 broadcast_in_dim.72
  99.6 0.3 copy-done.5
  99.9 0.7 tanh_add_fusion.1
  100.6 0.2 copy.13
  100.8 7.4 %fusion.4 = f32[128,128]{1,0:T(8,128)S(1)} fusion(f32[128,16,128]{2,1,0:T(8,128)S(1)} %bitcast.137, f32[128,128,128]{2,1,0:T(8,128)S(1)} %copy-done), kind=kOutput, calls=%fused_computation.30 | convolution fusion | flops 402898944 | bytes 9502720 | tf_op jit(solution)/shard_map/bpc,bcd->bpd/dot_general | solution.py:50
  108.2 4.4 %collective-permute-start.5 = (f32[1,64,128]{2,1,0:T(8,128)S(1)}, f32[1,64,128]{2,1,0:T(8,128)S(1)}, u32[]{:S(2)}, u32[]{:S(2)}) collective-permute-start(f32[1,64,128]{2,1,0:T(8,128)S(1)} %get-tuple-element.29), channel_id=1, source_target_pairs={{8,0},{16,8},{24,16},{32,24},{40,32},{48,40},{56,48},{64,56},{72,6... | collective-permute-start | bytes 98312 | tf_op jit(solution)/shard_map/ppermute | solution.py:21
  112.6 1.9 %collective-permute-start.4 = (f32[1,64,128]{2,1,0:T(8,128)S(1)}, f32[1,64,128]{2,1,0:T(8,128)S(1)}, u32[]{:S(2)}, u32[]{:S(2)}) collective-permute-start(f32[1,64,128]{2,1,0:T(8,128)S(1)} %get-tuple-element.28), channel_id=1, source_target_pairs={{0,8},{8,16},{16,24},{24,32},{32,40},{40,48},{48,56},{56,64},{64,7... | collective-permute-start | bytes 98312 | tf_op jit(solution)/shard_map/ppermute | solution.py:19
  114.5 0.1 add_tanh_fusion
  114.6 0.0 collective-permute-done.5
  114.6 4.7 %collective-permute-done.4 = f32[1,64,128]{2,1,0:T(8,128)S(1)} collective-permute-done((f32[1,64,128]{2,1,0:T(8,128)S(1)}, f32[1,64,128]{2,1,0:T(8,128)S(1)}, u32[]{:S(2)}, u32[]{:S(2)}) %collective-permute-start.4) | collective-permute-done | bytes 32800 | tf_op jit(solution)/shard_map/ppermute | solution.py:19
  119.4 4.2 %collective-permute-start.6 = (f32[34,1,128]{2,1,0:T(1,128)S(1)}, f32[34,1,128]{2,1,0:T(1,128)S(1)}, u32[]{:S(2)}, u32[]{:S(2)}) collective-permute-start(f32[34,1,128]{2,1,0:T(1,128)S(1)} %get-tuple-element.19), channel_id=1, source_target_pairs={{0,1},{1,2},{2,3},{3,4},{4,5},{5,6},{6,7},{8,9},{9,10},{10,11},{11... | collective-permute-start | bytes 52232 | tf_op jit(solution)/shard_map/ppermute | solution.py:19
  123.6 0.0 copy-start.3
  123.6 2.1 %collective-permute-start.7 = (f32[34,1,128]{2,1,0:T(1,128)S(1)}, f32[34,1,128]{2,1,0:T(1,128)S(1)}, u32[]{:S(2)}, u32[]{:S(2)}) collective-permute-start(f32[34,1,128]{2,1,0:T(1,128)S(1)} %get-tuple-element.20), channel_id=1, source_target_pairs={{1,0},{2,1},{3,2},{4,3},{5,4},{6,5},{7,6},{9,8},{10,9},{11,10},{12... | collective-permute-start | bytes 52232 | tf_op jit(solution)/shard_map/ppermute | solution.py:21
  125.6 0.2 pad_maximum_fusion.1
  125.9 1.0 fusion.26
  126.9 0.0 collective-permute-done.6
  126.9 1.9 %collective-permute-done.7 = f32[34,1,128]{2,1,0:T(1,128)S(1)} collective-permute-done((f32[34,1,128]{2,1,0:T(1,128)S(1)}, f32[34,1,128]{2,1,0:T(1,128)S(1)}, u32[]{:S(2)}, u32[]{:S(2)}) %collective-permute-start.7) | collective-permute-done | bytes 17440 | tf_op jit(solution)/shard_map/ppermute | solution.py:21
  128.8 0.2 maximum_maximum_fusion
  129.0 0.8 fusion.53
  129.8 1.0 fusion.9
  130.8 1.0 convolution_add_fusion.6
  131.8 1.0 convolution_add_fusion.5
  132.8 1.0 convolution_add_fusion.4
  133.7 1.0 convolution_add_fusion.3
  134.7 1.0 convolution_add_fusion.2
  135.7 1.0 convolution_add_fusion.1
  136.7 1.1 fusion
  137.8 0.2 broadcast_in_dim.76
  138.0 1.5 %tanh_add_fusion = f32[32,64,128]{2,1,0:T(8,128)} fusion(f32[32,64,128]{2,1,0:T(8,128)S(1)} %bitcast.134, f32[32,64,128]{2,1,0:T(8,128)S(1)} %bitcast.144, f32[32,64,128]{2,1,0:T(8,128)S(1)} %tanh_add_fusion.1, f32[128]{0:T(128)S(1)} %get-tuple-element.42, f32[128]{0:T(128)S(1)} %get-tuple-element.41, f32[128]{0:T(128)S(1)} %copy-done.5, ...), kind=kLoop, calls=%fused_computation.41 | loop fusion | flops 1572864 | bytes 4199936 | tf_op jit(solution)/shard_map/add | solution.py:109
  (19 shorter events, 0.1 us)
Async XLA Ops:
  6.5 74.4 %all-gather.2.cloned.1.call-start = ((), (), s32[]{:S(2)}) async-start(), calls=%async_computation | async-start | bytes 8454144 | tf_op jit(solution)/shard_map/all_gather | solution.py:75
  8.0 13.0 %collective-permute-start = (f32[1,64,128]{2,1,0:T(8,128)S(1)}, f32[1,64,128]{2,1,0:T(8,128)S(1)}, u32[]{:S(2)}, u32[]{:S(2)}) collective-permute-start(f32[1,64,128]{2,1,0:T(8,128)S(1)} %get-tuple-element.34), channel_id=1, source_target_pairs={{0,8},{8,16},{16,24},{24,32},{32,40},{40,48},{48,56},{56,64},{64,7... | collective-permute-start | bytes 98312 | tf_op jit(solution)/shard_map/ppermute | solution.py:19
  11.2 9.8 %collective-permute-start.1 = (f32[1,64,128]{2,1,0:T(8,128)S(1)}, f32[1,64,128]{2,1,0:T(8,128)S(1)}, u32[]{:S(2)}, u32[]{:S(2)}) collective-permute-start(f32[1,64,128]{2,1,0:T(8,128)S(1)} %get-tuple-element.33), channel_id=1, source_target_pairs={{8,0},{16,8},{24,16},{32,24},{40,32},{48,40},{56,48},{64,56},{72,6... | collective-permute-start | bytes 98312 | tf_op jit(solution)/shard_map/ppermute | solution.py:21
  17.6 3.5 %copy-start.1 = (f32[32,64,128]{2,1,0:T(8,128)S(1)}, f32[32,64,128]{2,1,0:T(8,128)}, u32[]{:S(2)}) copy-start(f32[32,64,128]{2,1,0:T(8,128)} %param.9) | copy-start | bytes 3145732
  21.1 6.6 %copy-start.2 = (f32[9,128,128]{2,1,0:T(8,128)S(1)}, f32[9,128,128]{2,1,0:T(8,128)}, u32[]{:S(2)}) copy-start(f32[9,128,128]{2,1,0:T(8,128)} %param.13) | copy-start | bytes 1769476
  21.5 8.2 %collective-permute-start.2 = (f32[34,1,128]{2,1,0:T(1,128)S(1)}, f32[34,1,128]{2,1,0:T(1,128)S(1)}, u32[]{:S(2)}, u32[]{:S(2)}) collective-permute-start(f32[34,1,128]{2,1,0:T(1,128)S(1)} %get-tuple-element.24), channel_id=1, source_target_pairs={{0,1},{1,2},{2,3},{3,4},{4,5},{5,6},{6,7},{8,9},{9,10},{10,11},{11... | collective-permute-start | bytes 52232 | tf_op jit(solution)/shard_map/ppermute | solution.py:19
  25.8 5.5 %collective-permute-start.3 = (f32[34,1,128]{2,1,0:T(1,128)S(1)}, f32[34,1,128]{2,1,0:T(1,128)S(1)}, u32[]{:S(2)}, u32[]{:S(2)}) collective-permute-start(f32[34,1,128]{2,1,0:T(1,128)S(1)} %get-tuple-element.25), channel_id=1, source_target_pairs={{1,0},{2,1},{3,2},{4,3},{5,4},{6,5},{7,6},{9,8},{10,9},{11,10},{12... | collective-permute-start | bytes 52232 | tf_op jit(solution)/shard_map/ppermute | solution.py:21
  88.7 10.6 %copy-start.4 = (f32[128]{0:T(128)S(1)}, f32[128]{0:T(128)}, u32[]{:S(2)}) copy-start(f32[128]{0:T(128)} %param.17) | copy-start | bytes 1540
  88.7 12.2 %copy-start = (f32[128,128,128]{2,1,0:T(8,128)S(1)}, f32[128,128,128]{2,1,0:T(8,128)}, u32[]{:S(2)}) copy-start(f32[128,128,128]{2,1,0:T(8,128)} %gather_fusion) | copy-start | bytes 25165828
  99.2 0.7 copy-start.5
  108.2 6.4 %collective-permute-start.5 = (f32[1,64,128]{2,1,0:T(8,128)S(1)}, f32[1,64,128]{2,1,0:T(8,128)S(1)}, u32[]{:S(2)}, u32[]{:S(2)}) collective-permute-start(f32[1,64,128]{2,1,0:T(8,128)S(1)} %get-tuple-element.29), channel_id=1, source_target_pairs={{8,0},{16,8},{24,16},{32,24},{40,32},{48,40},{56,48},{64,56},{72,6... | collective-permute-start | bytes 98312 | tf_op jit(solution)/shard_map/ppermute | solution.py:21
  112.6 6.8 %collective-permute-start.4 = (f32[1,64,128]{2,1,0:T(8,128)S(1)}, f32[1,64,128]{2,1,0:T(8,128)S(1)}, u32[]{:S(2)}, u32[]{:S(2)}) collective-permute-start(f32[1,64,128]{2,1,0:T(8,128)S(1)} %get-tuple-element.28), channel_id=1, source_target_pairs={{0,8},{8,16},{16,24},{24,32},{32,40},{40,48},{48,56},{56,64},{64,7... | collective-permute-start | bytes 98312 | tf_op jit(solution)/shard_map/ppermute | solution.py:19
  119.4 7.5 %collective-permute-start.6 = (f32[34,1,128]{2,1,0:T(1,128)S(1)}, f32[34,1,128]{2,1,0:T(1,128)S(1)}, u32[]{:S(2)}, u32[]{:S(2)}) collective-permute-start(f32[34,1,128]{2,1,0:T(1,128)S(1)} %get-tuple-element.19), channel_id=1, source_target_pairs={{0,1},{1,2},{2,3},{3,4},{4,5},{5,6},{6,7},{8,9},{9,10},{10,11},{11... | collective-permute-start | bytes 52232 | tf_op jit(solution)/shard_map/ppermute | solution.py:19
  123.6 2.3 %copy-start.3 = (f32[9,128,128]{2,1,0:T(8,128)S(1)}, f32[9,128,128]{2,1,0:T(8,128)}, u32[]{:S(2)}) copy-start(f32[9,128,128]{2,1,0:T(8,128)} %param.13) | copy-start | bytes 1769476
  123.6 5.2 %collective-permute-start.7 = (f32[34,1,128]{2,1,0:T(1,128)S(1)}, f32[34,1,128]{2,1,0:T(1,128)S(1)}, u32[]{:S(2)}, u32[]{:S(2)}) collective-permute-start(f32[34,1,128]{2,1,0:T(1,128)S(1)} %get-tuple-element.20), channel_id=1, source_target_pairs={{1,0},{2,1},{3,2},{4,3},{5,4},{6,5},{7,6},{9,8},{10,9},{11,10},{12... | collective-permute-start | bytes 52232 | tf_op jit(solution)/shard_map/ppermute | solution.py:21
Sparse Core Ops, SparseCore 0:
  10.3 70.6 all-gather.1
where the time goes:
time: 147 us; the launch traced here: 146 us
  waiting for transfers between devices  50.7 us (34%)
  matrix products  35.7 us (24%)
  starting transfers between devices  26 us (18%)
  between operations  13.9 us (9%)
  local copies, waits for them, and re-layouts  13 us (9%)
  other arithmetic  7.12 us (5%)
    all_gather x1, waiting for transfers between devices, per_device(): all_weights = lax.all_gather(read_weight, ('gx', 'gy'), axis=0, tiled=True)  41.7 us
    dot_general x2, matrix products, reader_head(): jnp.einsum(form, cell_vals, weight, precision=precise)  17.9 us
    dot_general x18, matrix products, per_device(): jnp.dot(shifted, conv_weight[tap_index], precision=precise, preferred_ele...  17.8 us
    ppermute x4, starting transfers between devices, padded_2(): lax.ppermute(tail, axis, [(i, (i + 1) % count) for i in range(ends)])  13.5 us
    ppermute x4, starting transfers between devices, padded_2(): lax.ppermute(head, axis, [((i + 1) % count, i) for i in range(ends)])  12.5 us
    gather x1, local copies, waits for them, and re-layouts, per_device(): all_weights.reshape(device_count, channels, channels)[reader_ids]  7.68 us
    ppermute x4, waiting for transfers between devices, padded_2(): lax.ppermute(tail, axis, [(i, (i + 1) % count) for i in range(ends)])  4.74 us
    ppermute x4, waiting for transfers between devices, padded_2(): lax.ppermute(head, axis, [((i + 1) % count, i) for i in range(ends)])  3.48 us
  transfers between devices with their start and end apart: 9, of which 4 were waited for; matrix products, arithmetic and copies ran while one was open for 12% of the time, Pallas kernels for 0%

commit v1 on v0

--- a/solution.py
+++ b/solution.py
@@ -72,7 +72,8 @@
     gy_count = lax.axis_size("gy")
     device_count = gx_count * gy_count
     reader_ids = readers[:, 0]
-    all_weights = lax.all_gather(read_weight, ("gx", "gy"), axis=0, tiled=True)
+    sent = jnp.stack([read_weight] * lax.axis_size(("gx", "gy")))
+    all_weights = jnp.concatenate(lax.all_to_all(sent, ("gx", "gy"), 0, 0), axis=0)
     block_weights = all_weights.reshape(device_count, channels, channels)[reader_ids]
     field = state
     for round_index in range(ROUNDS):

time: 147 us -> 184 us (1.25)
  waiting for transfers between devices: 50.7 us -> 84.1 us
  starting transfers between devices: 26 us -> 42.1 us
  between operations: 13.9 us -> 0.59 us
  other arithmetic: 7.12 us -> 4.16 us
  local copies, waits for them, and re-layouts: 13 us -> 15.3 us
    ppermute x4, waiting for transfers between devices: 4.74 us -> 79.7 us  [padded_2(): lax.ppermute(tail, axis, [(i, (i + 1) % count) for i in range(ends)])]
    all_gather x1 -> x0, waiting for transfers between devices: 41.7 us -> none  [per_device(): all_weights = lax.all_gather(read_weight, ('gx', 'gy'), axis=0, tiled=True)]
    all_to_all x0 -> x1, starting transfers between devices: none -> 11 us  [per_device(): lax.all_to_all(sent, ('gx', 'gy'), 0, 0)]
    another operation x0 -> x1, local copies, waits for them, and re-layouts: none -> 5.1 us  [per_device(): sent = jnp.stack([read_weight] * lax.axis_size(('gx', 'gy')))]
    ppermute x4, starting transfers between devices: 13.5 us -> 17.5 us  [padded_2(): lax.ppermute(tail, axis, [(i, (i + 1) % count) for i in range(ends)])]
  transfers between devices with their start and end apart: 9 -> 9, of which waited for: 4 -> 4; matrix products, arithmetic and copies ran while one was open for 12% -> 11% of each run, Pallas kernels for 0% -> 0%
where the time goes in v1:
time: 184 us; the launch traced here: 182 us
  waiting for transfers between devices  84.1 us (46%)
  starting transfers between devices  42.1 us (23%)
  matrix products  35.8 us (19%)
  local copies, waits for them, and re-layouts  15.3 us (8%)
  other arithmetic  4.16 us (2%)
    ppermute x4, waiting for transfers between devices, padded_2(): lax.ppermute(tail, axis, [(i, (i + 1) % count) for i in range(ends)])  79.7 us
    dot_general x2, matrix products, reader_head(): jnp.einsum(form, cell_vals, weight, precision=precise)  18 us
    dot_general x18, matrix products, per_device(): jnp.dot(shifted, conv_weight[tap_index], precision=precise, preferred_ele...  17.8 us
    ppermute x4, starting transfers between devices, padded_2(): lax.ppermute(tail, axis, [(i, (i + 1) % count) for i in range(ends)])  17.5 us
    ppermute x4, starting transfers between devices, padded_2(): lax.ppermute(head, axis, [((i + 1) % count, i) for i in range(ends)])  13.7 us
    all_to_all x1, starting transfers between devices, per_device(): lax.all_to_all(sent, ('gx', 'gy'), 0, 0)  11 us
    gather x1, local copies, waits for them, and re-layouts, per_device(): all_weights.reshape(device_count, channels, channels)[reader_ids]  7.68 us
    another operation x1, local copies, waits for them, and re-layouts, per_device(): sent = jnp.stack([read_weight] * lax.axis_size(('gx', 'gy')))  5.1 us
  transfers between devices with their start and end apart: 9, of which 4 were waited for; matrix products, arithmetic and copies ran while one was open for 11% of the time, Pallas kernels for 0%

profile of v1, /device:TPU:33, one launch (start us, length us, event | category | flops | bytes accessed | tf_op | source)
XLA Modules:
  0.0 182.0 jit_solution(9173233125770669361)
XLA Ops:
  0.0 5.1 %stack.2 = f32[128,128,128]{2,1,0:T(8,128)} broadcast(f32[128,128]{1,0:T(8,128)} %param.16), dimensions={1,2} | broadcast | bytes 8454144 | tf_op jit(solution)/shard_map/stack | solution.py:75
  5.1 0.0 copy-start.4
  5.1 11.0 %all-to-all-start = ((f32[128,128,128]{2,1,0:T(8,128)}), f32[128,128,128]{2,1,0:T(8,128)}, u32[]{:S(2)}, u32[]{:S(2)}) async-start(f32[128,128,128]{2,1,0:T(8,128)} %stack.2), calls=%async_computation | async-start | bytes 16777216 | tf_op jit(solution)/shard_map/all_to_all | solution.py:76
  16.1 0.0 copy-done.1
  16.1 4.2 %collective-permute-start.1 = (f32[1,64,128]{2,1,0:T(8,128)S(1)}, f32[1,64,128]{2,1,0:T(8,128)S(1)}, u32[]{:S(2)}, u32[]{:S(2)}) collective-permute-start(f32[1,64,128]{2,1,0:T(8,128)S(1)} %get-tuple-element.33), channel_id=1, source_target_pairs={{8,0},{16,8},{24,16},{32,24},{40,32},{48,40},{56,48},{64,56},{72,6... | collective-permute-start | bytes 98312 | tf_op jit(solution)/shard_map/ppermute | solution.py:21
  20.4 1.9 %collective-permute-start = (f32[1,64,128]{2,1,0:T(8,128)S(1)}, f32[1,64,128]{2,1,0:T(8,128)S(1)}, u32[]{:S(2)}, u32[]{:S(2)}) collective-permute-start(f32[1,64,128]{2,1,0:T(8,128)S(1)} %get-tuple-element.34), channel_id=1, source_target_pairs={{0,8},{8,16},{16,24},{24,32},{32,40},{40,48},{48,56},{56,64},{64,7... | collective-permute-start | bytes 98312 | tf_op jit(solution)/shard_map/ppermute | solution.py:19
  22.3 0.0 copy-done.9
  22.3 0.0 copy-done.8
  22.4 0.1 broadcast_in_dim.73
  22.5 0.2 gt.35
  22.7 0.1 broadcast_in_dim.66
  22.8 0.2 gt.32
  22.9 0.2 copy.12
  23.1 79.7 %collective-permute-done = f32[1,64,128]{2,1,0:T(8,128)S(1)} collective-permute-done((f32[1,64,128]{2,1,0:T(8,128)S(1)}, f32[1,64,128]{2,1,0:T(8,128)S(1)}, u32[]{:S(2)}, u32[]{:S(2)}) %collective-permute-start) | collective-permute-done | bytes 32800 | tf_op jit(solution)/shard_map/ppermute | solution.py:19
  102.9 1.3 collective-permute-done.1
  104.1 0.3 pad_maximum_fusion.6
  104.5 9.8 %collective-permute-start.2 = (f32[34,1,128]{2,1,0:T(1,128)S(1)}, f32[34,1,128]{2,1,0:T(1,128)S(1)}, u32[]{:S(2)}, u32[]{:S(2)}) collective-permute-start(f32[34,1,128]{2,1,0:T(1,128)S(1)} %get-tuple-element.24), channel_id=1, source_target_pairs={{0,1},{1,2},{2,3},{3,4},{4,5},{5,6},{6,7},{8,9},{9,10},{10,11},{11... | collective-permute-start | bytes 52232 | tf_op jit(solution)/shard_map/ppermute | solution.py:19
  114.3 2.1 %collective-permute-start.3 = (f32[34,1,128]{2,1,0:T(1,128)S(1)}, f32[34,1,128]{2,1,0:T(1,128)S(1)}, u32[]{:S(2)}, u32[]{:S(2)}) collective-permute-start(f32[34,1,128]{2,1,0:T(1,128)S(1)} %get-tuple-element.25), channel_id=1, source_target_pairs={{1,0},{2,1},{3,2},{4,3},{5,4},{6,5},{7,6},{9,8},{10,9},{11,10},{12... | collective-permute-start | bytes 52232 | tf_op jit(solution)/shard_map/ppermute | solution.py:21
  116.4 1.0 fusion.28
  117.4 1.0 fusion.14
  118.4 0.0 collective-permute-done.2
  118.4 1.0 collective-permute-done.3
  119.4 0.9 pad_maximum_fusion.5
  120.3 1.0 fusion.11
  121.3 1.0 convolution_add_fusion.12
  122.3 1.0 convolution_add_fusion.11
  123.3 1.0 convolution_add_fusion.10
  124.2 1.0 convolution_add_fusion.9
  125.2 1.0 convolution_add_fusion.8
  126.2 1.1 fusion.2
  127.3 0.0 all-to-all-done
  127.3 7.7 %gather_fusion = f32[128,128,128]{2,1,0:T(8,128)} fusion(f32[128,128,128]{2,1,0:T(8,128)} %all-to-all-done, s32[1024]{0:T(1024)S(1)} %pad_clamp_fusion), kind=kCustom, calls=%fused_computation | custom fusion | bytes 16777728 | tf_op jit(solution)/shard_map/gather | solution.py:77
  135.0 10.6 %fusion.3 = f32[128,128]{1,0:T(8,128)S(1)} fusion(f32[128,128,128]{2,1,0:T(8,128)} %gather_fusion, f32[128,16,128]{2,1,0:T(8,128)S(1)} %bitcast.130), kind=kOutput, calls=%fused_computation.29 | convolution fusion | flops 402898944 | bytes 9502720 | tf_op jit(solution)/shard_map/bpc,bcd->bpd/dot_general | solution.py:50
  145.6 0.0 copy-start.7
  145.6 0.1 add_tanh_fusion.1
  145.7 0.2 broadcast_in_dim.72
  146.0 0.3 copy-done.7
  146.2 0.7 tanh_add_fusion.1
  147.0 2.1 %collective-permute-start.4 = (f32[1,64,128]{2,1,0:T(8,128)S(1)}, f32[1,64,128]{2,1,0:T(8,128)S(1)}, u32[]{:S(2)}, u32[]{:S(2)}) collective-permute-start(f32[1,64,128]{2,1,0:T(8,128)S(1)} %get-tuple-element.28), channel_id=1, source_target_pairs={{0,8},{8,16},{16,24},{24,32},{32,40},{40,48},{48,56},{56,64},{64,7... | collective-permute-start | bytes 98312 | tf_op jit(solution)/shard_map/ppermute | solution.py:19
  149.1 5.3 %collective-permute-start.5 = (f32[1,64,128]{2,1,0:T(8,128)S(1)}, f32[1,64,128]{2,1,0:T(8,128)S(1)}, u32[]{:S(2)}, u32[]{:S(2)}) collective-permute-start(f32[1,64,128]{2,1,0:T(8,128)S(1)} %get-tuple-element.29), channel_id=1, source_target_pairs={{8,0},{16,8},{24,16},{32,24},{40,32},{48,40},{56,48},{64,56},{72,6... | collective-permute-start | bytes 98312 | tf_op jit(solution)/shard_map/ppermute | solution.py:21
  154.4 0.2 copy.13
  154.6 7.4 %fusion.4 = f32[128,128]{1,0:T(8,128)S(1)} fusion(f32[128,16,128]{2,1,0:T(8,128)S(1)} %bitcast.135, f32[128,128,128]{2,1,0:T(8,128)S(1)} %copy-done), kind=kOutput, calls=%fused_computation.30 | convolution fusion | flops 402898944 | bytes 9502720 | tf_op jit(solution)/shard_map/bpc,bcd->bpd/dot_general | solution.py:50
  162.0 0.1 add_tanh_fusion
  162.1 0.0 collective-permute-done.4
  162.1 0.0 collective-permute-done.5
  162.1 3.7 %collective-permute-start.6 = (f32[34,1,128]{2,1,0:T(1,128)S(1)}, f32[34,1,128]{2,1,0:T(1,128)S(1)}, u32[]{:S(2)}, u32[]{:S(2)}) collective-permute-start(f32[34,1,128]{2,1,0:T(1,128)S(1)} %get-tuple-element.19), channel_id=1, source_target_pairs={{0,1},{1,2},{2,3},{3,4},{4,5},{5,6},{6,7},{8,9},{9,10},{10,11},{11... | collective-permute-start | bytes 52232 | tf_op jit(solution)/shard_map/ppermute | solution.py:19
  165.8 0.0 copy-start.3
  165.8 2.1 %collective-permute-start.7 = (f32[34,1,128]{2,1,0:T(1,128)S(1)}, f32[34,1,128]{2,1,0:T(1,128)S(1)}, u32[]{:S(2)}, u32[]{:S(2)}) collective-permute-start(f32[34,1,128]{2,1,0:T(1,128)S(1)} %get-tuple-element.20), channel_id=1, source_target_pairs={{1,0},{2,1},{3,2},{4,3},{5,4},{6,5},{7,6},{9,8},{10,9},{11,10},{12... | collective-permute-start | bytes 52232 | tf_op jit(solution)/shard_map/ppermute | solution.py:21
  167.9 0.2 pad_maximum_fusion.1
  168.1 1.0 fusion.26
  169.1 0.0 collective-permute-done.6
  169.1 2.1 %collective-permute-done.7 = f32[34,1,128]{2,1,0:T(1,128)S(1)} collective-permute-done((f32[34,1,128]{2,1,0:T(1,128)S(1)}, f32[34,1,128]{2,1,0:T(1,128)S(1)}, u32[]{:S(2)}, u32[]{:S(2)}) %collective-permute-start.7) | collective-permute-done | bytes 17440 | tf_op jit(solution)/shard_map/ppermute | solution.py:21
  171.2 0.2 maximum_maximum_fusion
  171.4 0.8 fusion.53
  172.2 1.0 fusion.9
  173.2 1.0 convolution_add_fusion.6
  174.2 1.0 convolution_add_fusion.5
  175.2 1.0 convolution_add_fusion.4
  176.2 1.0 convolution_add_fusion.3
  177.2 1.0 convolution_add_fusion.2
  178.2 1.0 convolution_add_fusion.1
  179.2 1.1 fusion
  180.3 0.2 broadcast_in_dim.76
  180.5 1.5 tanh_add_fusion
  (27 shorter events, 0.2 us)
Async XLA Ops:
  5.1 11.0 %copy-start.1 = (f32[32,64,128]{2,1,0:T(8,128)S(1)}, f32[32,64,128]{2,1,0:T(8,128)}, u32[]{:S(2)}) copy-start(f32[32,64,128]{2,1,0:T(8,128)} %param.9) | copy-start | bytes 3145732
  5.1 17.2 %copy-start.9 = (s32[128,1]{0,1:T(1,128)S(1)}, s32[128,1]{0,1:T(1,128)}, u32[]{:S(2)}) copy-start(s32[128,1]{0,1:T(1,128)} %param.12) | copy-start | bytes 1540
  5.1 17.2 %copy-start.8 = (f32[2,128]{1,0:T(2,128)S(1)}, f32[2,128]{1,0:T(2,128)}, u32[]{:S(2)}) copy-start(f32[2,128]{1,0:T(2,128)} %param.14) | copy-start | bytes 3076
  5.1 17.2 %copy-start.5 = (s32[2,8,16]{2,1,0:T(8,128)S(1)}, s32[2,8,16]{2,1,0:T(8,128)}, u32[]{:S(2)}) copy-start(s32[2,8,16]{2,1,0:T(8,128)} %param.11) | copy-start | bytes 3076
  5.1 17.3 %copy-start.4 = (s32[2,32,64]{2,1,0:T(8,128)S(1)}, s32[2,32,64]{2,1,0:T(8,128)}, u32[]{:S(2)}) copy-start(s32[2,32,64]{2,1,0:T(8,128)} %param.10) | copy-start | bytes 49156
  5.1 122.2 %all-to-all-start = ((f32[128,128,128]{2,1,0:T(8,128)}), f32[128,128,128]{2,1,0:T(8,128)}, u32[]{:S(2)}, u32[]{:S(2)}) async-start(f32[128,128,128]{2,1,0:T(8,128)} %stack.2), calls=%async_computation | async-start | bytes 16777216 | tf_op jit(solution)/shard_map/all_to_all | solution.py:76
  16.1 88.0 %collective-permute-start.1 = (f32[1,64,128]{2,1,0:T(8,128)S(1)}, f32[1,64,128]{2,1,0:T(8,128)S(1)}, u32[]{:S(2)}, u32[]{:S(2)}) collective-permute-start(f32[1,64,128]{2,1,0:T(8,128)S(1)} %get-tuple-element.33), channel_id=1, source_target_pairs={{8,0},{16,8},{24,16},{32,24},{40,32},{48,40},{56,48},{64,56},{72,6... | collective-permute-start | bytes 98312 | tf_op jit(solution)/shard_map/ppermute | solution.py:21
  20.4 82.5 %collective-permute-start = (f32[1,64,128]{2,1,0:T(8,128)S(1)}, f32[1,64,128]{2,1,0:T(8,128)S(1)}, u32[]{:S(2)}, u32[]{:S(2)}) collective-permute-start(f32[1,64,128]{2,1,0:T(8,128)S(1)} %get-tuple-element.34), channel_id=1, source_target_pairs={{0,8},{8,16},{16,24},{24,32},{32,40},{40,48},{48,56},{56,64},{64,7... | collective-permute-start | bytes 98312 | tf_op jit(solution)/shard_map/ppermute | solution.py:19
  102.9 13.6 %copy-start.2 = (f32[9,128,128]{2,1,0:T(8,128)S(1)}, f32[9,128,128]{2,1,0:T(8,128)}, u32[]{:S(2)}) copy-start(f32[9,128,128]{2,1,0:T(8,128)} %param.13) | copy-start | bytes 1769476
  104.5 13.9 %collective-permute-start.2 = (f32[34,1,128]{2,1,0:T(1,128)S(1)}, f32[34,1,128]{2,1,0:T(1,128)S(1)}, u32[]{:S(2)}, u32[]{:S(2)}) collective-permute-start(f32[34,1,128]{2,1,0:T(1,128)S(1)} %get-tuple-element.24), channel_id=1, source_target_pairs={{0,1},{1,2},{2,3},{3,4},{4,5},{5,6},{6,7},{8,9},{9,10},{10,11},{11... | collective-permute-start | bytes 52232 | tf_op jit(solution)/shard_map/ppermute | solution.py:19
  114.3 5.1 %collective-permute-start.3 = (f32[34,1,128]{2,1,0:T(1,128)S(1)}, f32[34,1,128]{2,1,0:T(1,128)S(1)}, u32[]{:S(2)}, u32[]{:S(2)}) collective-permute-start(f32[34,1,128]{2,1,0:T(1,128)S(1)} %get-tuple-element.25), channel_id=1, source_target_pairs={{1,0},{2,1},{3,2},{4,3},{5,4},{6,5},{7,6},{9,8},{10,9},{11,10},{12... | collective-permute-start | bytes 52232 | tf_op jit(solution)/shard_map/ppermute | solution.py:21
  135.0 10.6 %copy-start.6 = (f32[128]{0:T(128)S(1)}, f32[128]{0:T(128)}, u32[]{:S(2)}) copy-start(f32[128]{0:T(128)} %param.17) | copy-start | bytes 1540
  135.0 19.6 %copy-start = (f32[128,128,128]{2,1,0:T(8,128)S(1)}, f32[128,128,128]{2,1,0:T(8,128)}, u32[]{:S(2)}) copy-start(f32[128,128,128]{2,1,0:T(8,128)} %gather_fusion) | copy-start | bytes 25165828
  145.6 0.7 copy-start.7
  147.0 15.1 %collective-permute-start.4 = (f32[1,64,128]{2,1,0:T(8,128)S(1)}, f32[1,64,128]{2,1,0:T(8,128)S(1)}, u32[]{:S(2)}, u32[]{:S(2)}) collective-permute-start(f32[1,64,128]{2,1,0:T(8,128)S(1)} %get-tuple-element.28), channel_id=1, source_target_pairs={{0,8},{8,16},{16,24},{24,32},{32,40},{40,48},{48,56},{56,64},{64,7... | collective-permute-start | bytes 98312 | tf_op jit(solution)/shard_map/ppermute | solution.py:19
  149.1 13.0 %collective-permute-start.5 = (f32[1,64,128]{2,1,0:T(8,128)S(1)}, f32[1,64,128]{2,1,0:T(8,128)S(1)}, u32[]{:S(2)}, u32[]{:S(2)}) collective-permute-start(f32[1,64,128]{2,1,0:T(8,128)S(1)} %get-tuple-element.29), channel_id=1, source_target_pairs={{8,0},{16,8},{24,16},{32,24},{40,32},{48,40},{56,48},{64,56},{72,6... | collective-permute-start | bytes 98312 | tf_op jit(solution)/shard_map/ppermute | solution.py:21
  162.1 7.0 %collective-permute-start.6 = (f32[34,1,128]{2,1,0:T(1,128)S(1)}, f32[34,1,128]{2,1,0:T(1,128)S(1)}, u32[]{:S(2)}, u32[]{:S(2)}) collective-permute-start(f32[34,1,128]{2,1,0:T(1,128)S(1)} %get-tuple-element.19), channel_id=1, source_target_pairs={{0,1},{1,2},{2,3},{3,4},{4,5},{5,6},{6,7},{8,9},{9,10},{10,11},{11... | collective-permute-start | bytes 52232 | tf_op jit(solution)/shard_map/ppermute | solution.py:19
  165.8 2.3 %copy-start.3 = (f32[9,128,128]{2,1,0:T(8,128)S(1)}, f32[9,128,128]{2,1,0:T(8,128)}, u32[]{:S(2)}) copy-start(f32[9,128,128]{2,1,0:T(8,128)} %param.13) | copy-start | bytes 1769476
  165.8 5.4 %collective-permute-start.7 = (f32[34,1,128]{2,1,0:T(1,128)S(1)}, f32[34,1,128]{2,1,0:T(1,128)S(1)}, u32[]{:S(2)}, u32[]{:S(2)}) collective-permute-start(f32[34,1,128]{2,1,0:T(1,128)S(1)} %get-tuple-element.20), channel_id=1, source_target_pairs={{1,0},{2,1},{3,2},{4,3},{5,4},{6,5},{7,6},{9,8},{10,9},{11,10},{12... | collective-permute-start | bytes 52232 | tf_op jit(solution)/shard_map/ppermute | solution.py:21
